TPU v7x, 32 devices: a whole 2x2x4 slice. The times are simulated.
32 devices in a mesh: row: 4 (over y, core), col: 8 (over z, x).
Axes of the slice: x: 2, y: 2, z: 4, core: 2. Of those that a mesh axis runs over, the one named last changes fastest.
Arguments:
- constraint_blocks: float32 [16, 16, 256, 256], P('row', 'col'), may hold values from -0.09375 to 0.09375
- factor_blocks: float32 [16, 16, 256, 256], P('row', 'col'), may hold values from -0.09375 to 0.09375
- band_offsets: int32 [8, 2], P('col'), may hold values from 0 to 63, as said below
- block_pattern: int32 [16, 16], P('row', 'col'), may hold values 0 or 1
- cost_linear: float32 [131072], P('col'), may hold values from -6 to 6
- cost_diagonal: float32 [131072], P('col'), may hold values from 0.5 to 4
- lower: float32 [4096], P('row'), may hold values from -1.5 to -0.2
- upper: float32 [4096], P('row'), may hold values from 0.2 to 1.5
- x_start: float32 [131072], P('col'), may hold values from -6 to 6
- z_start: float32 [4096], P('row'), may hold values from -1 to 1
- y_start: float32 [4096], P('row'), may hold values from -0.6 to 0.6
Outputs:
- x_final: float32 [131072], P('col')
- z_final: float32 [4096], P('row')
- y_final: float32 [4096], P('row')
- residuals: float32 [2, 2], replicated
Inputs may be any that keep to these rules, and one draw needn't show every extreme that they name: In each row of band_offsets the 2 offsets are distinct.
All inputs are finite; a program needn't handle non-finite values. No bound on the sum of `block_pattern` on one device may be relied on, other than what follows from the above.
Results may differ from a plain program's by a relative error of at most 0.00016.
Values sent between devices are 32-bit elements; how exact they have to be, the bound alone decides.
A program may use at most 64 MiB of HBM per device.

v0:
```python
import jax
import jax.numpy as jnp
from jax import lax
from jax.sharding import PartitionSpec as P

BS = 256
ITERS = 2
CG_STEPS = 2


sigma_shift = 1e-06
rho_step = 0.1
relaxation = 1.6


def local(
    constraint_blocks,
    factor_blocks,
    band_offsets,
    block_pattern,
    cost_linear,
    cost_diagonal,
    lower,
    upper,
    x_start,
    z_start,
    y_start,
):
    col_blocks = cost_linear.shape[0] // BS
    row_blocks = lower.shape[0] // BS
    first_row = lax.axis_index("row") * row_blocks
    block_rows = first_row + jnp.arange(row_blocks, dtype=jnp.int32)
    columns = (block_rows[:, None] % col_blocks + band_offsets[0][None, :]) % col_blocks
    selector = (
        columns[:, :, None] == jnp.arange(col_blocks, dtype=jnp.int32)[None, None, :]
    ).astype(jnp.float32)
    selector = selector * block_pattern.astype(jnp.float32)[:, :, None]
    shifted = cost_diagonal + sigma_shift

    def forward(blocks, vector):
        vector_blocks = vector.reshape(col_blocks, BS)
        gathered = jnp.einsum(
            "tkc,cb->tkb", selector, vector_blocks, precision=lax.Precision.HIGHEST
        )
        result = jnp.einsum("tkab,tkb->ta", blocks, gathered, precision=lax.Precision.HIGHEST)
        return result.reshape(-1)

    def backward(blocks, vector):
        vector_blocks = vector.reshape(row_blocks, BS)
        contrib = jnp.einsum("tkab,ta->tkb", blocks, vector_blocks, precision=lax.Precision.HIGHEST)
        result = jnp.einsum("tkc,tkb->cb", selector, contrib, precision=lax.Precision.HIGHEST)
        return result.reshape(-1)

    def images(iterate):
        return lax.psum(
            (forward(factor_blocks, iterate), forward(constraint_blocks, iterate)), "col"
        )

    recorded = []

    def record(iterate, z_value, constraint_image, dual_part):
        primal_local = jnp.max(jnp.abs(constraint_image - z_value))
        dual_local = jnp.max(jnp.abs(cost_diagonal * iterate + cost_linear + dual_part))
        recorded.append(lax.pmax((primal_local, dual_local), ("row", "col")))

    iterate, z_value, y_value = (x_start, z_start, y_start)
    for outer in range(ITERS):
        factor_image, constraint_image = images(iterate)
        gtg_local = backward(factor_blocks, factor_image)
        start_local = (
            backward(constraint_blocks, rho_step * z_value - y_value - rho_step * constraint_image)
            - gtg_local
        )
        if outer == 0:
            start_sum = lax.psum(start_local, "row")
        else:
            start_sum, dual_sum = lax.psum(
                (start_local, gtg_local + backward(constraint_blocks, y_value)), "row"
            )
            record(iterate, z_value, constraint_image, dual_sum)
        remainder = sigma_shift * iterate - cost_linear - shifted * iterate + start_sum
        solved = iterate
        tracked = constraint_image
        direction = jnp.zeros_like(remainder)
        factor_dir = jnp.zeros((row_blocks * BS,), jnp.float32)
        constraint_dir = jnp.zeros((row_blocks * BS,), jnp.float32)
        norm_old = jnp.float32(1.0)
        weighted_dir = jnp.float32(0.0)
        for inner in range(CG_STEPS):
            factor_rem, constraint_rem, norm_now, weighted_rem, weighted_mix = lax.psum(
                (
                    forward(factor_blocks, remainder),
                    forward(constraint_blocks, remainder),
                    jnp.sum(remainder * remainder),
                    jnp.sum(remainder * shifted * remainder),
                    jnp.sum(remainder * shifted * direction),
                ),
                "col",
            )
            ratio = norm_now / norm_old
            direction = remainder + ratio * direction
            factor_dir = factor_rem + ratio * factor_dir
            constraint_dir = constraint_rem + ratio * constraint_dir
            weighted_dir = weighted_rem + 2.0 * ratio * weighted_mix + ratio * ratio * weighted_dir
            image_part, squares = lax.psum(
                (
                    backward(factor_blocks, factor_dir)
                    + rho_step * backward(constraint_blocks, constraint_dir),
                    jnp.sum(factor_dir * factor_dir)
                    + rho_step * jnp.sum(constraint_dir * constraint_dir),
                ),
                "row",
            )
            image = image_part + shifted * direction
            step_size = norm_now / (squares + weighted_dir)
            solved = solved + step_size * direction
            remainder = remainder - step_size * image
            tracked = tracked + step_size * constraint_dir
            norm_old = norm_now
        iterate = relaxation * solved + (1.0 - relaxation) * iterate
        blended = relaxation * tracked + (1.0 - relaxation) * z_value
        z_new = jnp.minimum(jnp.maximum(blended + y_value / rho_step, lower), upper)
        y_value = y_value + rho_step * (blended - z_new)
        z_value = z_new
    factor_image, constraint_image = images(iterate)
    dual_sum = lax.psum(
        backward(factor_blocks, factor_image) + backward(constraint_blocks, y_value), "row"
    )
    record(iterate, z_value, constraint_image, dual_sum)
    primal_all = jnp.stack([pair[0] for pair in recorded])
    dual_all = jnp.stack([pair[1] for pair in recorded])
    residuals = jnp.stack([primal_all, dual_all])
    return (iterate, z_value, y_value, residuals)


def solution(mesh):
    placed = (
        P("row", "col", None, None),
        P("row", "col", None, None),
        P("col", None),
        P("row", "col"),
        P("col"),
        P("col"),
        P("row"),
        P("row"),
        P("col"),
        P("row"),
        P("row"),
    )
    return jax.shard_map(
        local,
        mesh=mesh,
        in_specs=placed,
        out_specs=(P("col"), P("row"), P("row"), P()),
        check_vma=False,
    )
```

profile of v0, /device:TPU:0, one launch (start us, length us, event | category | flops | bytes accessed | tf_op | source)
XLA Modules:
  0.0 444.9 jit_solution(5799026576622913540)
XLA Ops:
  9.9 3.4 fusion.78
  13.3 1.8 fusion.80
  15.2 23.4 %all-reduce.7 = (f32[4,256]{1,0:T(4,128)S(1)}, f32[1024]{0:T(1024)S(1)}) all-reduce(f32[4,256]{1,0:T(4,128)S(1)} %bitcast.264, f32[1024]{0:T(1024)S(1)} %bitcast.261), channel_id=1, replica_groups=mesh['row'=4,'col'=8] {'col'}, use_global_device_ids=true, to_apply=%region_1.2 | all-reduce | flops 2048 | bytes 16384 | tf_op jit(solution)/shard_map/psum | solution.py:55
  38.6 2.7 fusion.86
  41.4 1.1 fusion.162
  43.9 28.9 %all-reduce.15.cloned.1.call-done = f32[16384]{0:T(1024)} async-done(((f32[16384]{0:T(1024)}), f32[16384]{0:T(1024)}) %all-reduce.15.cloned.1.call-update) | async-done | bytes 65552 | tf_op jit(solution)/shard_map/psum | solution.py:75
  72.8 1.5 multiply_reduce_fusion.9
  74.5 1.8 fusion.74
  76.4 1.8 fusion.76
  78.2 22.5 %all-reduce.6 = (f32[1024]{0:T(1024)S(1)}, f32[]{:T(128)}, f32[1024]{0:T(1024)S(1)}, f32[]{:T(128)}, f32[]{:T(128)}) all-reduce(f32[1024]{0:T(1024)S(1)} %bitcast.253, f32[]{:T(128)} %get-tuple-element.17, f32[1024]{0:T(1024)S(1)} %bitcast.257, f32[]{:T(128)} %get-tuple-element.13, ...), channel_id=1, replica_groups=mesh['row'=4,'col'=8] {'col'}, use_global_device_ids=true, to_apply=%region_5.6 | all-reduce | flops 2051 | bytes 16408 | tf_op jit(solution)/shard_map/psum | solution.py:90
  102.0 1.1 fusion.164
  103.1 1.1 fusion.163
  106.9 6.6 %psum.258 = f32[]{:T(128)} all-reduce(f32[]{:T(128)S(6)} %add.317), channel_id=1, replica_groups=mesh['row'=4,'col'=8] {'row'}, use_global_device_ids=true, to_apply=%region_9.10 | all-reduce | flops 1 | bytes 8 | tf_op jit(solution)/shard_map/psum | solution.py:105
  118.0 15.6 %all-reduce.17.cloned.1.call-done = f32[16384]{0:T(1024)} async-done(((f32[16384]{0:T(1024)}), f32[16384]{0:T(1024)}) %all-reduce.17.cloned.1.call-update) | async-done | bytes 65552 | tf_op jit(solution)/shard_map/psum | solution.py:105
  133.6 1.5 multiply_reduce_fusion.6
  135.3 1.8 fusion.70
  137.1 1.8 fusion.72
  139.0 22.5 %all-reduce.5 = (f32[]{:T(128)}, f32[1024]{0:T(1024)S(1)}, f32[1024]{0:T(1024)S(1)}, f32[]{:T(128)}, f32[]{:T(128)}) all-reduce(f32[]{:T(128)} %get-tuple-element.16, f32[1024]{0:T(1024)S(1)} %bitcast.254, f32[1024]{0:T(1024)S(1)} %bitcast.258, f32[]{:T(128)} %get-tuple-element.11, ...), channel_id=1, replica_groups=mesh['row'=4,'col'=8] {'col'}, use_global_device_ids=true, to_apply=%region_16.17 | all-reduce | flops 2051 | bytes 16408 | tf_op jit(solution)/shard_map/psum | solution.py:90
  165.4 6.4 %psum.265 = f32[]{:T(128)} all-reduce(f32[]{:T(128)S(6)} %add.328), channel_id=1, replica_groups=mesh['row'=4,'col'=8] {'row'}, use_global_device_ids=true, to_apply=%region_21.22 | all-reduce | flops 1 | bytes 8 | tf_op jit(solution)/shard_map/psum | solution.py:105
  174.6 3.4 fusion.66
  178.0 1.8 fusion.68
  179.9 17.4 %all-reduce.4 = (f32[4,256]{1,0:T(4,128)S(1)}, f32[1024]{0:T(1024)S(1)}) all-reduce(f32[4,256]{1,0:T(4,128)S(1)} %bitcast.265, f32[1024]{0:T(1024)S(1)} %bitcast.262), channel_id=1, replica_groups=mesh['row'=4,'col'=8] {'col'}, use_global_device_ids=true, to_apply=%region_27.28 | all-reduce | flops 2048 | bytes 16384 | tf_op jit(solution)/shard_map/psum | solution.py:55
  197.3 2.7 fusion.84
  200.6 1.1 fusion.165
  203.3 1.1 fusion.168
  204.4 28.1 %all-reduce.19.cloned.1.call-done = f32[16384]{0:T(1024)} async-done(((f32[16384]{0:T(1024)}), f32[16384]{0:T(1024)}) %all-reduce.19.cloned.1.call-update) | async-done | bytes 65552 | tf_op jit(solution)/shard_map/psum | solution.py:77
  232.6 1.5 multiply_reduce_fusion.3
  234.3 1.8 fusion.62
  236.1 1.8 fusion.64
  238.0 22.5 %all-reduce.3 = (f32[1024]{0:T(1024)S(1)}, f32[]{:T(128)}, f32[1024]{0:T(1024)S(1)}, f32[]{:T(128)}, f32[]{:T(128)}) all-reduce(f32[1024]{0:T(1024)S(1)} %bitcast.255, f32[]{:T(128)} %get-tuple-element.15, f32[1024]{0:T(1024)S(1)} %bitcast.259, f32[]{:T(128)} %get-tuple-element.9, ...), channel_id=1, replica_groups=mesh['row'=4,'col'=8] {'col'}, use_global_device_ids=true, to_apply=%region_31.32 | all-reduce | flops 2051 | bytes 16408 | tf_op jit(solution)/shard_map/psum | solution.py:90
  263.4 1.1 fusion.166
  268.2 6.4 %psum.274 = f32[]{:T(128)} all-reduce(f32[]{:T(128)S(6)} %add.343), channel_id=1, replica_groups=mesh['row'=4,'col'=8] {'row'}, use_global_device_ids=true, to_apply=%region_35.36 | all-reduce | flops 1 | bytes 8 | tf_op jit(solution)/shard_map/psum | solution.py:105
  278.9 15.1 %all-reduce.21.cloned.1.call-done = f32[16384]{0:T(1024)} async-done(((f32[16384]{0:T(1024)}), f32[16384]{0:T(1024)}) %all-reduce.21.cloned.1.call-update) | async-done | bytes 65552 | tf_op jit(solution)/shard_map/psum | solution.py:105
  293.9 1.5 multiply_reduce_fusion
  295.7 1.8 fusion.58
  297.5 1.8 fusion.60
  299.4 22.5 %all-reduce.2 = (f32[]{:T(128)}, f32[1024]{0:T(1024)S(1)}, f32[1024]{0:T(1024)S(1)}, f32[]{:T(128)}, f32[]{:T(128)}) all-reduce(f32[]{:T(128)} %get-tuple-element.14, f32[1024]{0:T(1024)S(1)} %bitcast.256, f32[1024]{0:T(1024)S(1)} %bitcast.260, f32[]{:T(128)} %get-tuple-element.7, ...), channel_id=1, replica_groups=mesh['row'=4,'col'=8] {'col'}, use_global_device_ids=true, to_apply=%region_42.43 | all-reduce | flops 2051 | bytes 16408 | tf_op jit(solution)/shard_map/psum | solution.py:90
  325.6 6.7 %psum.281 = f32[]{:T(128)} all-reduce(f32[]{:T(128)S(6)} %add.354), channel_id=1, replica_groups=mesh['row'=4,'col'=8] {'row'}, use_global_device_ids=true, to_apply=%region_47.48 | all-reduce | flops 1 | bytes 8 | tf_op jit(solution)/shard_map/psum | solution.py:105
  335.2 3.4 fusion.54
  338.6 1.8 fusion.56
  340.4 17.4 %all-reduce.1 = (f32[4,256]{1,0:T(4,128)S(1)}, f32[1024]{0:T(1024)S(1)}) all-reduce(f32[4,256]{1,0:T(4,128)S(1)} %bitcast.266, f32[1024]{0:T(1024)S(1)} %bitcast.263), channel_id=1, replica_groups=mesh['row'=4,'col'=8] {'col'}, use_global_device_ids=true, to_apply=%region_60.61 | all-reduce | flops 2048 | bytes 16384 | tf_op jit(solution)/shard_map/psum | solution.py:55
  358.5 2.7 fusion.82
  361.2 1.1 fusion.169
  363.7 29.8 %all-reduce.23.cloned.1.call-done = (f32[16384]{0:T(1024)}, f32[16384]{0:T(1024)}) async-done(((f32[16384]{0:T(1024)}, f32[16384]{0:T(1024)}), (f32[16384]{0:T(1024)}, f32[16384]{0:T(1024)})) %all-reduce.23.cloned.1.call-update) | async-done | bytes 131088 | tf_op jit(solution)/shard_map/psum | solution.py:77
  393.4 1.6 abs_reduce_fusion.1
  395.0 39.6 %all-reduce = (f32[1]{0:T(128)}, f32[1]{0:T(128)}, f32[1]{0:T(128)}, f32[1]{0:T(128)}) all-reduce(f32[1]{0:T(128)} %bitcast.59, f32[1]{0:T(128)} %bitcast.51, f32[1]{0:T(128)} %bitcast.46, f32[1]{0:T(128)} %bitcast.43), channel_id=1, replica_groups=mesh['row'=4,'col'=8] {'row','col'}, use_global_device_ids=true, to_apply=%region_63.64 | all-reduce | flops 4 | bytes 32 | tf_op jit(solution)/shard_map/pmax | solution.py:64
  434.6 1.3 maximum_bitcast_fusion.1
  436.0 1.3 maximum_bitcast_fusion
  (119 shorter events, 19.9 us)
Async XLA Ops:
  7.2 6.1 %copy-start = (f32[4,2,256,256]{3,2,1,0:T(8,128)S(1)}, f32[4,2,256,256]{3,2,1,0:T(8,128)}, u32[]{:S(2)}) copy-start(f32[4,2,256,256]{3,2,1,0:T(8,128)} %param.11) | copy-start | bytes 6291460
  7.2 65.6 %all-reduce.15.cloned.1.call-start = ((), (), s32[]{:S(2)}) async-start(), calls=%async_computation | async-start | bytes 131072 | tf_op jit(solution)/shard_map/psum | solution.py:75
  13.3 28.0 %copy-start.11 = (f32[1024]{0:T(1024)S(1)}, f32[1024]{0:T(1024)}, u32[]{:S(2)}) copy-start(f32[1024]{0:T(1024)} %param.21) | copy-start | bytes 12292
  13.3 28.0 %copy-start.13 = (f32[1024]{0:T(1024)S(1)}, f32[1024]{0:T(1024)}, u32[]{:S(2)}) copy-start(f32[1024]{0:T(1024)} %param.20) | copy-start | bytes 12292
  38.6 34.2 %copy-start.7 = (f32[16384]{0:T(1024)S(1)}, f32[16384]{0:T(1024)}, u32[]{:S(2)}) copy-start(f32[16384]{0:T(1024)} %param.16) | copy-start | bytes 196612
  38.6 34.2 %copy-start.8 = (f32[16384]{0:T(1024)S(1)}, f32[16384]{0:T(1024)}, u32[]{:S(2)}) copy-start(f32[16384]{0:T(1024)} %param.15) | copy-start | bytes 196612
  38.6 34.2 %copy-start.9 = (f32[16384]{0:T(1024)S(1)}, f32[16384]{0:T(1024)}, u32[]{:S(2)}) copy-start(f32[16384]{0:T(1024)} %param.19) | copy-start | bytes 196612
  43.8 89.7 %all-reduce.17.cloned.1.call-start = ((), (), s32[]{:S(2)}) async-start(), calls=%async_computation.1 | async-start | bytes 131072 | tf_op jit(solution)/shard_map/psum | solution.py:105
  74.3 2.1 copy-start.1
  101.4 1.7 copy-start.2
  105.6 127.0 %all-reduce.19.cloned.1.call-start = ((), (), s32[]{:S(2)}) async-start(), calls=%async_computation.2 | async-start | bytes 131072 | tf_op jit(solution)/shard_map/psum | solution.py:77
  135.1 2.1 copy-start.3
  178.0 22.0 %copy-start.15 = (f32[1024]{0:T(1024)S(1)}, f32[1024]{0:T(1024)}, u32[]{:S(2)}) copy-start(f32[1024]{0:T(1024)} %param.18) | copy-start | bytes 12292
  178.0 22.0 %copy-start.16 = (f32[1024]{0:T(1024)S(1)}, f32[1024]{0:T(1024)}, u32[]{:S(2)}) copy-start(f32[1024]{0:T(1024)} %param.17) | copy-start | bytes 12292
  203.1 90.9 %all-reduce.21.cloned.1.call-start = ((), (), s32[]{:S(2)}) async-start(), calls=%async_computation.3 | async-start | bytes 131072 | tf_op jit(solution)/shard_map/psum | solution.py:105
  234.1 2.1 copy-start.4
  261.1 2.4 copy-start.5
  265.9 127.5 %all-reduce.23.cloned.1.call-start = ((), (), s32[]{:S(2)}) async-start(), calls=%async_computation.4 | async-start | bytes 262144 | tf_op jit(solution)/shard_map/psum | solution.py:77
  295.4 2.1 copy-start.6
  334.9 58.5 %copy-start.10 = (f32[16384]{0:T(1024)}, f32[16384]{0:T(1024)S(1)}, u32[]{:S(2)}) copy-start(f32[16384]{0:T(1024)S(1)} %multiply_add_fusion) | copy-start | bytes 196612
  358.5 3.8 copy-start.14
  361.2 76.7 %copy-start.12 = (f32[1024]{0:T(1024)}, f32[1024]{0:T(1024)S(1)}, u32[]{:S(2)}) copy-start(f32[1024]{0:T(1024)S(1)} %multiply_add_fusion.2) | copy-start | bytes 12292
Sparse Core Ops, SparseCore 0:
  44.0 28.7 all-reduce.14
  105.7 27.7 all-reduce.16
  203.2 29.3 all-reduce.18
  266.0 27.8 all-reduce.20
  363.8 29.5 all-reduce.22
where the time goes:
time: 454 us; the launch traced here: 445 us
  blocking collectives  214 us (47%)
  waiting for transfers between devices  118 us (26%)
  matrix products  52.4 us (12%)
  between operations  37.4 us (8%)
  other arithmetic  18.1 us (4%)
  local copies, waits for them, and re-layouts  5.2 us (1%)
    psum x4, blocking collectives, local(): lax.psum((forward(factor_blocks, remainder), forward(constraint_blocks, r...  90 us
    psum x3, blocking collectives, images(): lax.psum((forward(factor_blocks, iterate), forward(constraint_blocks, ite...  58.1 us
    psum x2, waiting for transfers between devices, local(): lax.psum((start_local, gtg_local + backward(constraint_blocks, y_value)),...  57.9 us
    pmax x1, blocking collectives, record(): recorded.append(lax.pmax((primal_local, dual_local), ('row', 'col')))  39.6 us
    psum x2, waiting for transfers between devices, local(): lax.psum((backward(factor_blocks, factor_dir) + rho_step * backward(const...  30.7 us
    dot_general x14, matrix products, forward(): jnp.einsum('tkab,tkb->ta', blocks, gathered, precision=lax.Precision.HIGH...  30.3 us
    psum x1, waiting for transfers between devices, local(): start_sum = lax.psum(start_local, 'row')  28.9 us
    psum x4, blocking collectives, local(): lax.psum((backward(factor_blocks, factor_dir) + rho_step * backward(const...  26 us
  transfers between devices with their start and end apart: 5, of which 5 were waited for; matrix products, arithmetic and copies ran while one was open for 0% of the time, Pallas kernels for 0%

commit v1 on v0

v1 whole, which is shorter than its diff:
```python
import functools

import jax
import jax.numpy as jnp
from jax import lax
from jax.experimental import pallas as pl
from jax.experimental.pallas import tpu as pltpu
from jax.sharding import PartitionSpec as P

ITERS = 2
CG_STEPS = 2
LANES = 128

sigma_shift = 1e-06
rho_step = 0.1
relaxation = 1.6

f32 = jnp.float32
bf16 = jnp.bfloat16


def kernel(
    n_row,
    n_col,
    a_blocks,
    g_blocks,
    offsets,
    pattern,
    q_ref,
    d_ref,
    lower_ref,
    upper_ref,
    x0_ref,
    z0_ref,
    y0_ref,
    x_ref,
    z_ref,
    y_ref,
    res_ref,
    f_hi,
    f_lo,
    r_ref,
    p_ref,
    s_ref,
    wide,
    col_buf,
    row_buf,
    col_send,
    col_recv,
    row_send,
    row_recv,
):
    row_blocks, bands, bs, _ = a_blocks.shape
    halves = bs // LANES
    tile = halves * row_blocks
    length = x0_ref.shape[0]
    col_blocks = length // halves
    my_row = lax.axis_index("row")
    my_col = lax.axis_index("col")

    barrier = pltpu.get_barrier_semaphore()
    for d in range(1, n_row):
        pl.semaphore_signal(barrier, inc=1, device_id={"row": lax.rem(my_row + d, n_row)})
    for d in range(1, n_col):
        pl.semaphore_signal(barrier, inc=1, device_id={"col": lax.rem(my_col + d, n_col)})

    for t in range(row_blocks):
        for k in range(bands):
            on = pattern[t, k].astype(f32)
            for m, blocks in enumerate((g_blocks, a_blocks)):
                value = blocks[t, k] * on
                high = value.astype(bf16)
                f_hi[t, m * bs : (m + 1) * bs, k * bs : (k + 1) * bs] = high
                f_lo[t, m * bs : (m + 1) * bs, k * bs : (k + 1) * bs] = (
                    value - high.astype(f32)
                ).astype(bf16)
    wide[...] = jnp.zeros_like(wide)
    pl.semaphore_wait(barrier, n_row + n_col - 2)

    line = lax.broadcasted_iota(jnp.int32, (8, bands * bs), 0)
    line_y = lax.broadcasted_iota(jnp.int32, (8, 2 * bs), 0)
    sends = []

    def stacked(rows, line):
        total = jnp.zeros(line.shape, f32)
        for i, value in enumerate(rows):
            high = value.astype(bf16).astype(f32)
            total = jnp.where(line == 2 * i, high, total)
            total = jnp.where(line == 2 * i + 1, value - high, total)
        return total.astype(bf16)

    def forward(ref, phase):
        for t in range(row_blocks):
            pieces = []
            for k in range(bands):
                c = lax.rem(my_row * row_blocks + t + offsets[0, k], col_blocks)
                for h in range(halves):
                    pieces.append(ref[pl.ds(c * halves + h, 1), :])
            lhs = stacked([jnp.concatenate(pieces, axis=1)], line)
            dims = (((1,), (1,)), ((), ()))
            out = lax.dot_general(lhs, f_hi[t], dims, preferred_element_type=f32)
            out = out + lax.dot_general(lhs, f_lo[t], dims, preferred_element_type=f32)
            out = out[0:1] + out[1:2]
            for m in range(2):
                for h in range(halves):
                    at = m * bs + h * LANES
                    row = m * tile + t * halves + h
                    col_buf[phase, my_col, row : row + 1, :] = out[:, at : at + LANES]

    def backward(vectors, phase):
        for t in range(row_blocks):
            rows = []
            for g, a in vectors:
                rows.append(
                    jnp.concatenate(
                        [v[t * halves + h : t * halves + h + 1] for v in (g, a) for h in range(halves)],
                        axis=1,
                    )
                )
            lhs = stacked(rows, line_y)
            out = jnp.dot(lhs, f_hi[t], preferred_element_type=f32)
            out = out + jnp.dot(lhs, f_lo[t], preferred_element_type=f32)
            for i in range(len(vectors)):
                value = out[2 * i : 2 * i + 1] + out[2 * i + 1 : 2 * i + 2]
                for k in range(bands):
                    for h in range(halves):
                        at = k * bs + h * LANES
                        row = t * halves + h
                        row_buf[phase, i * bands + k, my_row, row : row + 1, :] = value[
                            :, at : at + LANES
                        ]

    def exchange_col(phase):
        copies = []
        for d in range(1, n_col):
            mine = col_buf.at[phase, my_col]
            copies.append(
                pltpu.make_async_remote_copy(
                    src_ref=mine,
                    dst_ref=mine,
                    send_sem=col_send.at[phase, d],
                    recv_sem=col_recv.at[phase, d],
                    device_id={"col": lax.rem(my_col + d, n_col)},
                )
            )
            copies[-1].start()
        sends.extend(copies)
        for copy in copies:
            copy.wait_recv()

    def exchange_row(phase, first, last):
        copies = []
        for d in range(1, n_row):
            mine = row_buf.at[phase, pl.ds(first, last - first), my_row]
            copies.append(
                pltpu.make_async_remote_copy(
                    src_ref=mine,
                    dst_ref=mine,
                    send_sem=row_send.at[phase, d],
                    recv_sem=row_recv.at[phase, d],
                    device_id={"row": lax.rem(my_row + d, n_row)},
                )
            )
            copies[-1].start()
        sends.extend(copies)
        for copy in copies:
            copy.wait_recv()

    def col_sum(phase):
        total = col_buf[phase, 0]
        for i in range(1, n_col):
            total = total + col_buf[phase, i]
        return total

    extra = bands

    def plane_sum(phase):
        total = row_buf[phase, extra, 0]
        for i in range(1, n_row):
            total = total + row_buf[phase, extra, i]
        return jnp.sum(total, axis=(0, 1), keepdims=True)

    def expand(phase, i):
        total = None
        for k in range(bands):
            at = i * bands + k
            value = row_buf[phase, at].reshape(n_row * tile, LANES)
            wide[at, 0 : n_row * tile, :] = value
            wide[at, length : length + n_row * tile, :] = value
            start = length - halves * offsets[0, k]
            part = wide[at, pl.ds(start, length), :]
            total = part if total is None else total + part
        return total

    def lines(value):
        return jnp.sum(value, axis=0, keepdims=True)

    col_phase = 0
    row_phase = 0
    forward(x0_ref, col_phase)
    col_buf[col_phase, my_col, 2 * tile : 2 * tile + 8, :] = jnp.zeros((8, LANES), f32)
    exchange_col(col_phase)
    total = col_sum(col_phase)
    g, a = total[0:tile], total[tile : 2 * tile]
    col_phase += 1

    z, y = z0_ref[...], y0_ref[...]
    x_ref[...] = x0_ref[...]
    primal, dual = [], []

    def record(dual_sum):
        primal.append(jnp.max(jnp.abs(a - z), axis=0, keepdims=True))
        value = jnp.abs(d_ref[...] * x_ref[...] + q_ref[...] + dual_sum)
        dual.append(jnp.max(value, axis=0, keepdims=True))

    for outer in range(ITERS):
        vectors = [(-g, rho_step * z - y - rho_step * a)]
        if outer > 0:
            vectors.append((g, y))
        backward(vectors, row_phase)
        exchange_row(row_phase, 0, bands * len(vectors))
        start_sum = expand(row_phase, 0)
        if outer > 0:
            record(expand(row_phase, 1))
        row_phase += 1
        x = x_ref[...]
        shifted = d_ref[...] + sigma_shift
        r_ref[...] = sigma_shift * x - q_ref[...] - shifted * x + start_sum
        s_ref[...] = x
        g_s, a_s = g, a
        for inner in range(CG_STEPS):
            r = r_ref[...]
            weighted = (d_ref[...] + sigma_shift) * r
            col_buf[col_phase, my_col, 2 * tile : 2 * tile + 8, :] = jnp.zeros((8, LANES), f32)
            at = 2 * tile
            col_buf[col_phase, my_col, at : at + 1, :] = lines(r * r)
            col_buf[col_phase, my_col, at + 1 : at + 2, :] = lines(weighted * r)
            if inner > 0:
                col_buf[col_phase, my_col, at + 2 : at + 3, :] = lines(weighted * p_ref[...])
            forward(r_ref, col_phase)
            exchange_col(col_phase)
            total = col_sum(col_phase)
            col_phase += 1
            sums = jnp.sum(total[2 * tile : 2 * tile + 8], axis=1, keepdims=True)
            norm, w_rem, w_mix = sums[0:1], sums[1:2], sums[2:3]
            g_r, a_r = total[0:tile], total[tile : 2 * tile]
            if inner == 0:
                p_ref[...] = r
                g_d, a_d, w_dir = g_r, a_r, w_rem
            else:
                ratio = norm / norm_old
                p_ref[...] = r + ratio * p_ref[...]
                g_d = g_r + ratio * g_d
                a_d = a_r + ratio * a_d
                w_dir = w_rem + 2.0 * ratio * w_mix + ratio * ratio * w_dir
            row_buf[row_phase, extra, my_row] = g_d * g_d + rho_step * (a_d * a_d)
            if inner < CG_STEPS - 1:
                backward([(g_d, rho_step * a_d)], row_phase)
                exchange_row(row_phase, 0, extra + 1)
            else:
                exchange_row(row_phase, extra, extra + 1)
            alpha = norm / (plane_sum(row_phase) + w_dir)
            p = p_ref[...]
            s_ref[...] = s_ref[...] + alpha * p
            g_s = g_s + alpha * g_d
            a_s = a_s + alpha * a_d
            if inner < CG_STEPS - 1:
                image = expand(row_phase, 0) + (d_ref[...] + sigma_shift) * p
                r_ref[...] = r_ref[...] - alpha * image
            row_phase += 1
            norm_old = norm
        x_ref[...] = relaxation * s_ref[...] + (1.0 - relaxation) * x_ref[...]
        g = relaxation * g_s + (1.0 - relaxation) * g
        a = relaxation * a_s + (1.0 - relaxation) * a
        blended = relaxation * a_s + (1.0 - relaxation) * z
        z_new = jnp.minimum(jnp.maximum(blended + y / rho_step, lower_ref[...]), upper_ref[...])
        y = y + rho_step * (blended - z_new)
        z = z_new
    z_ref[...] = z
    y_ref[...] = y

    backward([(g, y)], row_phase)
    exchange_row(row_phase, 0, bands)
    record(expand(row_phase, 0))
    row_phase += 1

    found = primal + dual
    row_buf[row_phase, extra, my_row] = jnp.zeros((tile, LANES), f32)
    for i, value in enumerate(found):
        row_buf[row_phase, extra, my_row, i : i + 1, :] = value
    exchange_row(row_phase, extra, extra + 1)
    total = row_buf[row_phase, extra, 0]
    for i in range(1, n_row):
        total = jnp.maximum(total, row_buf[row_phase, extra, i])
    col_buf[col_phase, my_col] = jnp.concatenate([total, total, total], axis=0)
    exchange_col(col_phase)
    total = col_buf[col_phase, 0, 0:tile]
    for i in range(1, n_col):
        total = jnp.maximum(total, col_buf[col_phase, i, 0:tile])
    top = jnp.max(total, axis=1, keepdims=True)
    for i in range(len(found)):
        u, v = divmod(i, ITERS)
        res_ref[u : u + 1, v : v + 1] = top[i : i + 1]
    for copy in sends:
        copy.wait_send()


def solution(mesh):
    n_row, n_col = mesh.shape["row"], mesh.shape["col"]

    def local(a, g, offsets, pattern, q, d, lower, upper, x, z, y):
        row_blocks, bands, bs, _ = a.shape
        tile = row_blocks * bs // LANES
        length = x.shape[0] // LANES
        planes = 2 * bands
        col_phases = 2 + ITERS * CG_STEPS
        row_phases = ITERS * (CG_STEPS + 1) + 2
        flat = lambda v: v.reshape(-1, LANES)
        vmem = pl.BlockSpec(memory_space=pltpu.VMEM)
        smem = pl.BlockSpec(memory_space=pltpu.SMEM)
        out = pl.pallas_call(
            functools.partial(kernel, n_row, n_col),
            name="osqp",
            out_shape=(
                jax.ShapeDtypeStruct((length, LANES), f32),
                jax.ShapeDtypeStruct((tile, LANES), f32),
                jax.ShapeDtypeStruct((tile, LANES), f32),
                jax.ShapeDtypeStruct((2, ITERS), f32),
            ),
            in_specs=[vmem, vmem, smem, smem] + [vmem] * 7,
            out_specs=(vmem, vmem, vmem, vmem),
            scratch_shapes=[
                pltpu.VMEM((row_blocks, 2 * bs, bands * bs), bf16),
                pltpu.VMEM((row_blocks, 2 * bs, bands * bs), bf16),
                pltpu.VMEM((length, LANES), f32),
                pltpu.VMEM((length, LANES), f32),
                pltpu.VMEM((length, LANES), f32),
                pltpu.VMEM((2 * bands, 2 * length, LANES), f32),
                pltpu.VMEM((col_phases, n_col, 2 * tile + 8, LANES), f32),
                pltpu.VMEM((row_phases, planes, n_row, tile, LANES), f32),
                pltpu.SemaphoreType.DMA((col_phases, n_col)),
                pltpu.SemaphoreType.DMA((col_phases, n_col)),
                pltpu.SemaphoreType.DMA((row_phases, n_row)),
                pltpu.SemaphoreType.DMA((row_phases, n_row)),
            ],
            compiler_params=pltpu.CompilerParams(
                collective_id=0, has_side_effects=True, vmem_limit_bytes=48 << 20
            ),
        )(a, g, offsets, pattern, flat(q), flat(d), flat(lower), flat(upper), flat(x), flat(z), flat(y))
        return out[0].reshape(-1), out[1].reshape(-1), out[2].reshape(-1), out[3]

    placed = (
        P("row", "col", None, None),
        P("row", "col", None, None),
        P("col", None),
        P("row", "col"),
        P("col"),
        P("col"),
        P("row"),
        P("row"),
        P("col"),
        P("row"),
        P("row"),
    )
    return jax.shard_map(
        local,
        mesh=mesh,
        in_specs=placed,
        out_specs=(P("col"), P("row"), P("row"), P()),
        check_vma=False,
    )
```

time: 454 us -> 79.9 us (0.18); the launches traced: 445 us -> 79.4 us
  blocking collectives: 214 us -> 0 us
  waiting for transfers between devices: 118 us -> 0 us
  Pallas kernels: 0 us -> 66.5 us
  matrix products: 52.4 us -> 0 us
  between operations: 37.4 us -> 0.65 us
  other arithmetic: 18.1 us -> 0 us
  local copies, waits for them, and re-layouts: 5.2 us -> 12.2 us
    psum x11 -> x0, blocking collectives: 174 us -> none  [the longest x4 90 us: local(): lax.psum((forward(factor_blocks, remainder), forward(constraint_blocks, r...]
    psum x5 -> x0, waiting for transfers between devices: 117 us -> none  [the longest x2 57.9 us: local(): lax.psum((start_local, gtg_local + backward(constraint_blocks, y_value)),...]
    pallas_call x0 -> x1, Pallas kernels: none -> 66.5 us  [local(): pl.pallas_call(functools.partial(kernel, n_row, n_col), name='osqp', out_...]
    dot_general x43 -> x0, matrix products: 52.4 us -> none  [the longest x14 30.3 us: forward(): jnp.einsum('tkab,tkb->ta', blocks, gathered, precision=lax.Precision.HIGH...]
    pmax x1 -> x0, blocking collectives: 39.6 us -> none  [record(): recorded.append(lax.pmax((primal_local, dual_local), ('row', 'col')))]
    reduce_sum x11 -> x0, other arithmetic: 10.3 us -> none  [the longest x4 5.93 us: local(): jnp.sum(remainder * shifted * direction)]
    unnamed x51 -> x25, local copies, waits for them, and re-layouts: 4.17 us -> 12.2 us
  transfers between devices with their start and end apart: 5 -> 0, of which waited for: 5 -> 0; matrix products, arithmetic and copies ran while one was open for 0% -> 0% of each run, Pallas kernels for 0% -> 0%
where the time goes in v1:
time: 79.9 us; the launch traced here: 79.4 us
  Pallas kernels  66.5 us (83%)
  local copies, waits for them, and re-layouts  12.2 us (15%)
    pallas_call x1, Pallas kernels, local(): pl.pallas_call(functools.partial(kernel, n_row, n_col), name='osqp', out_...  66.5 us
    unnamed x25, local copies, waits for them, and re-layouts  12.2 us

profile of v1, /device:TPU:0, one launch (start us, length us, event | category | flops | bytes accessed | tf_op | source)
XLA Modules:
  0.0 79.4 jit_solution(6381593143588188413)
XLA Ops:
  0.6 0.8 copy.15.pattern
  1.4 0.0 copy-start
  1.4 1.6 %copy-done = f32[4,2,256,256]{3,2,1,0:T(8,128)S(1)} copy-done((f32[4,2,256,256]{3,2,1,0:T(8,128)S(1)}, f32[4,2,256,256]{3,2,1,0:T(8,128)}, u32[]{:S(2)}) %copy-start) | copy-done | bytes 2097176
  3.0 0.0 copy-start.1
  3.0 1.6 %copy-done.1 = f32[4,2,256,256]{3,2,1,0:T(8,128)S(1)} copy-done((f32[4,2,256,256]{3,2,1,0:T(8,128)S(1)}, f32[4,2,256,256]{3,2,1,0:T(8,128)}, u32[]{:S(2)}) %copy-start.1) | copy-done | bytes 2097176
  4.6 0.0 copy-start.2
  4.6 0.8 %copy-done.2 = f32[16384]{0:T(1024)S(1)} copy-done((f32[16384]{0:T(1024)S(1)}, f32[16384]{0:T(1024)}, u32[]{:S(2)}) %copy-start.2) | copy-done | bytes 65560
  5.4 0.0 copy-start.3
  5.4 0.8 %copy-done.3 = f32[16384]{0:T(1024)S(1)} copy-done((f32[16384]{0:T(1024)S(1)}, f32[16384]{0:T(1024)}, u32[]{:S(2)}) %copy-start.3) | copy-done | bytes 65560
  6.3 0.0 copy-start.4
  6.3 0.8 %copy-done.4 = f32[16384]{0:T(1024)S(1)} copy-done((f32[16384]{0:T(1024)S(1)}, f32[16384]{0:T(1024)}, u32[]{:S(2)}) %copy-start.4) | copy-done | bytes 65560
  7.1 0.0 copy-start.5
  7.1 0.7 copy-done.5
  7.8 0.0 copy-start.6
  7.8 0.7 copy-done.6
  8.5 0.0 copy-start.7
  8.5 0.7 copy-done.7
  9.2 0.0 copy-start.8
  9.2 0.7 copy-done.8
  9.8 0.0 copy-start.9
  9.9 0.7 copy-done.9
  10.5 66.5 %osqp.1 = (f32[128,128]{1,0:T(8,128)S(1)}, f32[8,128]{1,0:T(8,128)S(1)}, f32[8,128]{1,0:T(8,128)S(1)}, f32[2,2]{1,0:T(2,128)S(1)}) custom-call(f32[4,2,256,256]{3,2,1,0:T(8,128)S(1)} %copy-done, f32[4,2,256,256]{3,2,1,0:T(8,128)S(1)} %copy-done.1, s32[1,2]{1,0:T(1,128)S(1)} %copy-done.9, s32[4,2]{1,0:T(4,128)S(1)} %copy.15.pattern, f32[128,128]{1,0:T(8,128)S(1)} %bitcast.10, ...), custom_call_target="tpu_custom_call" | custom-call | tf_op jit(solution)/shard_map/osqp/pallas_call | solution.py:321
  77.1 0.6 copy.20
  77.7 0.6 copy.21
  78.3 0.6 copy.22
  78.9 0.6 copy.23
Async XLA Ops:
  1.4 1.6 %copy-start = (f32[4,2,256,256]{3,2,1,0:T(8,128)S(1)}, f32[4,2,256,256]{3,2,1,0:T(8,128)}, u32[]{:S(2)}) copy-start(f32[4,2,256,256]{3,2,1,0:T(8,128)} %a_blocks.1) | copy-start | bytes 6291460
  3.0 1.6 %copy-start.1 = (f32[4,2,256,256]{3,2,1,0:T(8,128)S(1)}, f32[4,2,256,256]{3,2,1,0:T(8,128)}, u32[]{:S(2)}) copy-start(f32[4,2,256,256]{3,2,1,0:T(8,128)} %g_blocks.1) | copy-start | bytes 6291460
  4.6 0.8 %copy-start.2 = (f32[16384]{0:T(1024)S(1)}, f32[16384]{0:T(1024)}, u32[]{:S(2)}) copy-start(f32[16384]{0:T(1024)} %param.15) | copy-start | bytes 196612
  5.4 0.8 %copy-start.3 = (f32[16384]{0:T(1024)S(1)}, f32[16384]{0:T(1024)}, u32[]{:S(2)}) copy-start(f32[16384]{0:T(1024)} %param.16) | copy-start | bytes 196612
  6.3 0.8 %copy-start.4 = (f32[16384]{0:T(1024)S(1)}, f32[16384]{0:T(1024)}, u32[]{:S(2)}) copy-start(f32[16384]{0:T(1024)} %param.19) | copy-start | bytes 196612
  7.1 0.7 copy-start.5
  7.8 0.7 copy-start.6
  8.5 0.7 copy-start.7
  9.2 0.7 copy-start.8
  9.8 0.7 copy-start.9

commit v2 on v1

--- a/solution.py
+++ b/solution.py
@@ -22,6 +22,21 @@
 def kernel(
     n_row,
     n_col,
+    a_hbm,
+    g_hbm,
+    offsets_hbm,
+    pattern_hbm,
+    q_hbm,
+    d_hbm,
+    lower_hbm,
+    upper_hbm,
+    x_hbm,
+    z_hbm,
+    y_hbm,
+    x_ref,
+    z_ref,
+    y_ref,
+    res_ref,
     a_blocks,
     g_blocks,
     offsets,
@@ -30,13 +45,8 @@
     d_ref,
     lower_ref,
     upper_ref,
-    x0_ref,
-    z0_ref,
-    y0_ref,
-    x_ref,
-    z_ref,
-    y_ref,
-    res_ref,
+    block_sem,
+    small_sem,
     f_hi,
     f_lo,
     r_ref,
@@ -53,10 +63,41 @@
     row_blocks, bands, bs, _ = a_blocks.shape
     halves = bs // LANES
     tile = halves * row_blocks
-    length = x0_ref.shape[0]
+    length = x_ref.shape[0]
     col_blocks = length // halves
     my_row = lax.axis_index("row")
     my_col = lax.axis_index("col")
+
+    small = [
+        pltpu.make_async_copy(src, dst, small_sem.at[i])
+        for i, (src, dst) in enumerate(
+            (
+                (pattern_hbm, pattern),
+                (offsets_hbm, offsets),
+                (x_hbm, x_ref),
+                (z_hbm, z_ref),
+                (y_hbm, y_ref),
+                (q_hbm, q_ref),
+                (d_hbm, d_ref),
+                (lower_hbm, lower_ref),
+                (upper_hbm, upper_ref),
+            )
+        )
+    ]
+    loads = [
+        [
+            pltpu.make_async_copy(src.at[t], dst.at[t], block_sem.at[t, m])
+            for m, (src, dst) in enumerate(((g_hbm, g_blocks), (a_hbm, a_blocks)))
+        ]
+        for t in range(row_blocks)
+    ]
+    for copy in small[:2]:
+        copy.start()
+    for pair in loads:
+        for copy in pair:
+            copy.start()
+    for copy in small[2:]:
+        copy.start()
 
     barrier = pltpu.get_barrier_semaphore()
     for d in range(1, n_row):
@@ -64,7 +105,12 @@
     for d in range(1, n_col):
         pl.semaphore_signal(barrier, inc=1, device_id={"col": lax.rem(my_col + d, n_col)})
 
+    wide[...] = jnp.zeros_like(wide)
+    for copy in small[:2]:
+        copy.wait()
     for t in range(row_blocks):
+        for copy in loads[t]:
+            copy.wait()
         for k in range(bands):
             on = pattern[t, k].astype(f32)
             for m, blocks in enumerate((g_blocks, a_blocks)):
@@ -74,7 +120,8 @@
                 f_lo[t, m * bs : (m + 1) * bs, k * bs : (k + 1) * bs] = (
                     value - high.astype(f32)
                 ).astype(bf16)
-    wide[...] = jnp.zeros_like(wide)
+    for copy in small[2:]:
+        copy.wait()
     pl.semaphore_wait(barrier, n_row + n_col - 2)
 
     line = lax.broadcasted_iota(jnp.int32, (8, bands * bs), 0)
@@ -130,10 +177,10 @@
                             :, at : at + LANES
                         ]
 
-    def exchange_col(phase):
+    def exchange_col(phase, rows):
         copies = []
         for d in range(1, n_col):
-            mine = col_buf.at[phase, my_col]
+            mine = col_buf.at[phase, my_col, pl.ds(0, rows)]
             copies.append(
                 pltpu.make_async_remote_copy(
                     src_ref=mine,
@@ -166,10 +213,10 @@
         for copy in copies:
             copy.wait_recv()
 
-    def col_sum(phase):
-        total = col_buf[phase, 0]
+    def col_sum(phase, first, last):
+        total = col_buf[phase, 0, first:last]
         for i in range(1, n_col):
-            total = total + col_buf[phase, i]
+            total = total + col_buf[phase, i, first:last]
         return total
 
     extra = bands
@@ -197,15 +244,13 @@
 
     col_phase = 0
     row_phase = 0
-    forward(x0_ref, col_phase)
-    col_buf[col_phase, my_col, 2 * tile : 2 * tile + 8, :] = jnp.zeros((8, LANES), f32)
-    exchange_col(col_phase)
-    total = col_sum(col_phase)
+    forward(x_ref, col_phase)
+    exchange_col(col_phase, 2 * tile)
+    total = col_sum(col_phase, 0, 2 * tile)
     g, a = total[0:tile], total[tile : 2 * tile]
     col_phase += 1
 
-    z, y = z0_ref[...], y0_ref[...]
-    x_ref[...] = x0_ref[...]
+    z, y = z_ref[...], y_ref[...]
     primal, dual = [], []
 
     def record(dual_sum):
@@ -231,24 +276,25 @@
         for inner in range(CG_STEPS):
             r = r_ref[...]
             weighted = (d_ref[...] + sigma_shift) * r
-            col_buf[col_phase, my_col, 2 * tile : 2 * tile + 8, :] = jnp.zeros((8, LANES), f32)
             at = 2 * tile
+            used = 2 if inner == 0 else 3
             col_buf[col_phase, my_col, at : at + 1, :] = lines(r * r)
             col_buf[col_phase, my_col, at + 1 : at + 2, :] = lines(weighted * r)
             if inner > 0:
                 col_buf[col_phase, my_col, at + 2 : at + 3, :] = lines(weighted * p_ref[...])
             forward(r_ref, col_phase)
-            exchange_col(col_phase)
-            total = col_sum(col_phase)
+            exchange_col(col_phase, at + used)
+            total = col_sum(col_phase, 0, at)
+            sums = jnp.sum(col_sum(col_phase, at, at + used), axis=1, keepdims=True)
             col_phase += 1
-            sums = jnp.sum(total[2 * tile : 2 * tile + 8], axis=1, keepdims=True)
-            norm, w_rem, w_mix = sums[0:1], sums[1:2], sums[2:3]
+            norm, w_rem = sums[0:1], sums[1:2]
             g_r, a_r = total[0:tile], total[tile : 2 * tile]
             if inner == 0:
                 p_ref[...] = r
                 g_d, a_d, w_dir = g_r, a_r, w_rem
             else:
                 ratio = norm / norm_old
+                w_mix = sums[2:3]
                 p_ref[...] = r + ratio * p_ref[...]
                 g_d = g_r + ratio * g_d
                 a_d = a_r + ratio * a_d
@@ -292,8 +338,8 @@
     total = row_buf[row_phase, extra, 0]
     for i in range(1, n_row):
         total = jnp.maximum(total, row_buf[row_phase, extra, i])
-    col_buf[col_phase, my_col] = jnp.concatenate([total, total, total], axis=0)
-    exchange_col(col_phase)
+    col_buf[col_phase, my_col, 0:tile] = total
+    exchange_col(col_phase, tile)
     total = col_buf[col_phase, 0, 0:tile]
     for i in range(1, n_col):
         total = jnp.maximum(total, col_buf[col_phase, i, 0:tile])
@@ -317,7 +363,7 @@
         row_phases = ITERS * (CG_STEPS + 1) + 2
         flat = lambda v: v.reshape(-1, LANES)
         vmem = pl.BlockSpec(memory_space=pltpu.VMEM)
-        smem = pl.BlockSpec(memory_space=pltpu.SMEM)
+        hbm = pl.BlockSpec(memory_space=pltpu.HBM)
         out = pl.pallas_call(
             functools.partial(kernel, n_row, n_col),
             name="osqp",
@@ -327,9 +373,19 @@
                 jax.ShapeDtypeStruct((tile, LANES), f32),
                 jax.ShapeDtypeStruct((2, ITERS), f32),
             ),
-            in_specs=[vmem, vmem, smem, smem] + [vmem] * 7,
+            in_specs=[hbm] * 11,
             out_specs=(vmem, vmem, vmem, vmem),
             scratch_shapes=[
+                pltpu.VMEM(a.shape, f32),
+                pltpu.VMEM(g.shape, f32),
+                pltpu.SMEM(offsets.shape, jnp.int32),
+                pltpu.SMEM(pattern.shape, jnp.int32),
+                pltpu.VMEM((length, LANES), f32),
+                pltpu.VMEM((length, LANES), f32),
+                pltpu.VMEM((tile, LANES), f32),
+                pltpu.VMEM((tile, LANES), f32),
+                pltpu.SemaphoreType.DMA((row_blocks, 2)),
+                pltpu.SemaphoreType.DMA((9,)),
                 pltpu.VMEM((row_blocks, 2 * bs, bands * bs), bf16),
                 pltpu.VMEM((row_blocks, 2 * bs, bands * bs), bf16),
                 pltpu.VMEM((length, LANES), f32),
@@ -344,7 +400,7 @@
                 pltpu.SemaphoreType.DMA((row_phases, n_row)),
             ],
             compiler_params=pltpu.CompilerParams(
-                collective_id=0, has_side_effects=True, vmem_limit_bytes=48 << 20
+                collective_id=0, has_side_effects=True, vmem_limit_bytes=56 << 20
             ),
         )(a, g, offsets, pattern, flat(q), flat(d), flat(lower), flat(upper), flat(x), flat(z), flat(y))
         return out[0].reshape(-1), out[1].reshape(-1), out[2].reshape(-1), out[3]

time: 79.9 us -> 72.8 us (0.911)
  local copies, waits for them, and re-layouts: 12.2 us -> 6.6 us
  Pallas kernels: 66.5 us -> 65.3 us
    unnamed x25 -> x5, local copies, waits for them, and re-layouts: 12.2 us -> 6.6 us
    pallas_call x1, Pallas kernels: 66.5 us -> 65.3 us  [local(): pl.pallas_call(functools.partial(kernel, n_row, n_col), name='osqp', out_...]
where the time goes in v2:
time: 72.8 us; the launch traced here: 72.5 us
  Pallas kernels  65.3 us (90%)
  local copies, waits for them, and re-layouts  6.6 us (9%)
    pallas_call x1, Pallas kernels, local(): pl.pallas_call(functools.partial(kernel, n_row, n_col), name='osqp', out_...  65.3 us
    unnamed x5, local copies, waits for them, and re-layouts  6.6 us

profile of v2, /device:TPU:0, one launch (start us, length us, event | category | flops | bytes accessed | tf_op | source)
XLA Modules:
  0.0 72.5 jit_solution(17257633456269863534)
XLA Ops:
  0.6 1.3 %copy.15.pattern_hbm = s32[4,2]{1,0:T(4,128)} copy(s32[4,2]{0,1:T(2,128)} %param.14) | data formatting | bytes 64 | tf_op args[3]
  2.0 65.3 %osqp.1 = (f32[128,128]{1,0:T(8,128)}, f32[8,128]{1,0:T(8,128)}, f32[8,128]{1,0:T(8,128)}, f32[2,2]{1,0:T(2,128)}) custom-call(f32[4,2,256,256]{3,2,1,0:T(8,128)} %a_hbm.1, f32[4,2,256,256]{3,2,1,0:T(8,128)} %g_hbm.1, s32[1,2]{1,0:T(1,128)} %offsets_hbm.1, s32[4,2]{1,0:T(4,128)} %copy.15.pattern_hbm, f32[128,128]{1,0:T(8,128)} %bitcast.10, ...), custom_call_target="tpu_custom_call" | custom-call | tf_op jit(solution)/shard_map/osqp/pallas_call | solution.py:367
  67.3 1.5 %copy.20 = f32[16384]{0:T(1024)} copy(f32[16384]{0:T(1024)} %bitcast.13) | data formatting | bytes 131072
  68.7 1.3 %copy.21 = f32[1024]{0:T(1024)} copy(f32[1024]{0:T(1024)} %bitcast.15) | data formatting | bytes 8192
  70.0 1.3 %copy.22 = f32[1024]{0:T(1024)} copy(f32[1024]{0:T(1024)} %bitcast.14) | data formatting | bytes 8192
  71.3 1.2 %copy.23 = f32[2,2]{1,0:T(2,128)} copy(f32[2,2]{1,0:T(2,128)} %get-tuple-element.19) | data formatting | bytes 32

commit v3 on v2

--- a/solution.py
+++ b/solution.py
@@ -17,6 +17,24 @@
 
 f32 = jnp.float32
 bf16 = jnp.bfloat16
+
+
+def far_first(n):
+    return sorted(range(1, n), key=lambda d: -min(d, n - d))
+
+
+def hand_over(*refs):
+    n = (len(refs) - 1) // 3
+    sources, targets, held, sem = refs[:n], refs[n : 2 * n], refs[2 * n : 3 * n], refs[-1]
+    inward = [pltpu.make_async_copy(sources[i], held[i], sem.at[0, i]) for i in range(n)]
+    outward = [pltpu.make_async_copy(held[i], targets[i], sem.at[1, i]) for i in range(n)]
+    for copy in inward:
+        copy.start()
+    for i in range(n):
+        inward[i].wait()
+        outward[i].start()
+    for copy in outward:
+        copy.wait()
 
 
 def kernel(
@@ -112,7 +130,7 @@
         for copy in loads[t]:
             copy.wait()
         for k in range(bands):
-            on = pattern[t, k].astype(f32)
+            on = pattern[k, t].astype(f32)
             for m, blocks in enumerate((g_blocks, a_blocks)):
                 value = blocks[t, k] * on
                 high = value.astype(bf16)
@@ -179,7 +197,7 @@
 
     def exchange_col(phase, rows):
         copies = []
-        for d in range(1, n_col):
+        for d in far_first(n_col):
             mine = col_buf.at[phase, my_col, pl.ds(0, rows)]
             copies.append(
                 pltpu.make_async_remote_copy(
@@ -197,7 +215,7 @@
 
     def exchange_row(phase, first, last):
         copies = []
-        for d in range(1, n_row):
+        for d in far_first(n_row):
             mine = row_buf.at[phase, pl.ds(first, last - first), my_row]
             copies.append(
                 pltpu.make_async_remote_copy(
@@ -253,10 +271,9 @@
     z, y = z_ref[...], y_ref[...]
     primal, dual = [], []
 
-    def record(dual_sum):
-        primal.append(jnp.max(jnp.abs(a - z), axis=0, keepdims=True))
+    def dual_max(dual_sum):
         value = jnp.abs(d_ref[...] * x_ref[...] + q_ref[...] + dual_sum)
-        dual.append(jnp.max(value, axis=0, keepdims=True))
+        return jnp.max(value, axis=0, keepdims=True)
 
     for outer in range(ITERS):
         vectors = [(-g, rho_step * z - y - rho_step * a)]
@@ -266,7 +283,8 @@
         exchange_row(row_phase, 0, bands * len(vectors))
         start_sum = expand(row_phase, 0)
         if outer > 0:
-            record(expand(row_phase, 1))
+            primal.append(jnp.max(jnp.abs(a - z), axis=0, keepdims=True))
+            dual.append(dual_max(expand(row_phase, 1)))
         row_phase += 1
         x = x_ref[...]
         shifted = d_ref[...] + sigma_shift
@@ -326,27 +344,25 @@
     y_ref[...] = y
 
     backward([(g, y)], row_phase)
-    exchange_row(row_phase, 0, bands)
-    record(expand(row_phase, 0))
-    row_phase += 1
-
-    found = primal + dual
+    primal.append(jnp.max(jnp.abs(a - z), axis=0, keepdims=True))
     row_buf[row_phase, extra, my_row] = jnp.zeros((tile, LANES), f32)
-    for i, value in enumerate(found):
+    for i, value in enumerate(primal):
         row_buf[row_phase, extra, my_row, i : i + 1, :] = value
-    exchange_row(row_phase, extra, extra + 1)
+    exchange_row(row_phase, 0, extra + 1)
+    dual.append(dual_max(expand(row_phase, 0)))
     total = row_buf[row_phase, extra, 0]
     for i in range(1, n_row):
         total = jnp.maximum(total, row_buf[row_phase, extra, i])
-    col_buf[col_phase, my_col, 0:tile] = total
-    exchange_col(col_phase, tile)
-    total = col_buf[col_phase, 0, 0:tile]
+    for i, value in enumerate(dual):
+        col_buf[col_phase, my_col, i : i + 1, :] = value
+    exchange_col(col_phase, ITERS)
+    found = col_buf[col_phase, 0, 0:ITERS]
     for i in range(1, n_col):
-        total = jnp.maximum(total, col_buf[col_phase, i, 0:tile])
-    top = jnp.max(total, axis=1, keepdims=True)
-    for i in range(len(found)):
-        u, v = divmod(i, ITERS)
-        res_ref[u : u + 1, v : v + 1] = top[i : i + 1]
+        found = jnp.maximum(found, col_buf[col_phase, i, 0:ITERS])
+    for u, value in enumerate((total[0:ITERS], found)):
+        top = jnp.max(value, axis=1, keepdims=True)
+        for v in range(ITERS):
+            res_ref[u : u + 1, v : v + 1] = top[v : v + 1]
     for copy in sends:
         copy.wait_send()
 
@@ -360,7 +376,7 @@
         length = x.shape[0] // LANES
         planes = 2 * bands
         col_phases = 2 + ITERS * CG_STEPS
-        row_phases = ITERS * (CG_STEPS + 1) + 2
+        row_phases = ITERS * (CG_STEPS + 1) + 1
         flat = lambda v: v.reshape(-1, LANES)
         vmem = pl.BlockSpec(memory_space=pltpu.VMEM)
         hbm = pl.BlockSpec(memory_space=pltpu.HBM)
@@ -379,7 +395,7 @@
                 pltpu.VMEM(a.shape, f32),
                 pltpu.VMEM(g.shape, f32),
                 pltpu.SMEM(offsets.shape, jnp.int32),
-                pltpu.SMEM(pattern.shape, jnp.int32),
+                pltpu.SMEM(pattern.shape[::-1], jnp.int32),
                 pltpu.VMEM((length, LANES), f32),
                 pltpu.VMEM((length, LANES), f32),
                 pltpu.VMEM((tile, LANES), f32),
@@ -402,7 +418,16 @@
             compiler_params=pltpu.CompilerParams(
                 collective_id=0, has_side_effects=True, vmem_limit_bytes=56 << 20
             ),
-        )(a, g, offsets, pattern, flat(q), flat(d), flat(lower), flat(upper), flat(x), flat(z), flat(y))
+        )(a, g, offsets, pattern.T, flat(q), flat(d), flat(lower), flat(upper), flat(x), flat(z), flat(y))
+        out = pl.pallas_call(
+            hand_over,
+            name="hand_over",
+            out_shape=tuple(jax.ShapeDtypeStruct(v.shape, v.dtype) for v in out),
+            in_specs=[hbm] * len(out),
+            out_specs=(hbm,) * len(out),
+            scratch_shapes=[pltpu.VMEM(v.shape, v.dtype) for v in out]
+            + [pltpu.SemaphoreType.DMA((2, len(out)))],
+        )(*out)
         return out[0].reshape(-1), out[1].reshape(-1), out[2].reshape(-1), out[3]
 
     placed = (

time: 72.8 us -> 66.5 us (0.913)
  local copies, waits for them, and re-layouts: 6.6 us -> 0 us
    unnamed x5 -> x0, local copies, waits for them, and re-layouts: 6.6 us -> none
    pallas_call x0 -> x1, Pallas kernels: none -> 1.55 us  [local(): pl.pallas_call(hand_over, name='hand_over', out_shape=tuple((jax.ShapeDty...]
    pallas_call x1, Pallas kernels: 65.3 us -> 64.2 us  [local(): pl.pallas_call(functools.partial(kernel, n_row, n_col), name='osqp', out_...]
where the time goes in v3:
time: 66.5 us; the launch traced here: 66.3 us
  Pallas kernels  65.7 us (99%)
    pallas_call x1, Pallas kernels, local(): pl.pallas_call(functools.partial(kernel, n_row, n_col), name='osqp', out_...  64.2 us
    pallas_call x1, Pallas kernels, local(): pl.pallas_call(hand_over, name='hand_over', out_shape=tuple((jax.ShapeDty...  1.55 us

profile of v3, /device:TPU:0, one launch (start us, length us, event | category | flops | bytes accessed | tf_op | source)
XLA Modules:
  0.0 66.3 jit_solution(1036777843011391400)
XLA Ops:
  0.6 64.2 %osqp.1 = (f32[128,128]{1,0:T(8,128)}, f32[8,128]{1,0:T(8,128)}, f32[8,128]{1,0:T(8,128)}, f32[2,2]{1,0:T(2,128)}) custom-call(f32[4,2,256,256]{3,2,1,0:T(8,128)} %a_hbm.1, f32[4,2,256,256]{3,2,1,0:T(8,128)} %g_hbm.1, s32[1,2]{1,0:T(1,128)} %offsets_hbm.1, s32[2,4]{1,0:T(2,128)} %bitcast.18, f32[128,128]{1,0:T(8,128)} %bitcast.11, f32[128,128]{1,0:T(8,128)} %bitcast.12, ...), custom_call_target="tpu_custom_call" | custom-call | tf_op jit(solution)/shard_map/osqp/pallas_call | solution.py:383
  64.8 1.5 %hand_over.1 = (f32[128,128]{1,0:T(8,128)}, f32[8,128]{1,0:T(8,128)}, f32[8,128]{1,0:T(8,128)}, f32[2,2]{1,0:T(2,128)}) custom-call(f32[128,128]{1,0:T(8,128)} %get-tuple-element.12.refs_0_, f32[8,128]{1,0:T(8,128)} %get-tuple-element.13.refs_1_, f32[8,128]{1,0:T(8,128)} %get-tuple-element.14.refs_2_, f32[2,2]{1,0:T(2,128)} %get-tuple-element.15.refs_3_), custom_call_target="tpu_custom_call" | custom-call | tf_op jit(solution)/shard_map/hand_over/pallas_call | solution.py:422

commit v4 on v3

--- a/solution.py
+++ b/solution.py
@@ -154,25 +154,32 @@
             total = jnp.where(line == 2 * i + 1, value - high, total)
         return total.astype(bf16)
 
-    def forward(ref, phase):
+    def forward(ref, phase, used):
+        lhs = []
         for t in range(row_blocks):
             pieces = []
             for k in range(bands):
                 c = lax.rem(my_row * row_blocks + t + offsets[0, k], col_blocks)
                 for h in range(halves):
                     pieces.append(ref[pl.ds(c * halves + h, 1), :])
-            lhs = stacked([jnp.concatenate(pieces, axis=1)], line)
-            dims = (((1,), (1,)), ((), ()))
-            out = lax.dot_general(lhs, f_hi[t], dims, preferred_element_type=f32)
-            out = out + lax.dot_general(lhs, f_lo[t], dims, preferred_element_type=f32)
-            out = out[0:1] + out[1:2]
-            for m in range(2):
-                for h in range(halves):
-                    at = m * bs + h * LANES
-                    row = m * tile + t * halves + h
-                    col_buf[phase, my_col, row : row + 1, :] = out[:, at : at + LANES]
+            lhs.append(stacked([jnp.concatenate(pieces, axis=1)], line))
+        dims = (((1,), (1,)), ((), ()))
+        copies = []
+        for m in range(2):
+            rows = []
+            for t in range(row_blocks):
+                high, low = (f[t, m * bs : (m + 1) * bs, :] for f in (f_hi, f_lo))
+                out = lax.dot_general(lhs[t], high, dims, preferred_element_type=f32)
+                out = out + lax.dot_general(lhs[t], low, dims, preferred_element_type=f32)
+                out = out[0:1] + out[1:2]
+                rows.extend(out[:, h * LANES : (h + 1) * LANES] for h in range(halves))
+            col_buf[phase, my_col, m * tile : (m + 1) * tile, :] = jnp.concatenate(rows, axis=0)
+            copies.extend(start_col(phase, m, m * tile, tile + m * used))
+        for copy in copies:
+            copy.wait_recv()
 
     def backward(vectors, phase):
+        lhs = []
         for t in range(row_blocks):
             rows = []
             for g, a in vectors:
@@ -182,36 +189,37 @@
                         axis=1,
                     )
                 )
-            lhs = stacked(rows, line_y)
-            out = jnp.dot(lhs, f_hi[t], preferred_element_type=f32)
-            out = out + jnp.dot(lhs, f_lo[t], preferred_element_type=f32)
-            for i in range(len(vectors)):
-                value = out[2 * i : 2 * i + 1] + out[2 * i + 1 : 2 * i + 2]
-                for k in range(bands):
+            lhs.append(stacked(rows, line_y))
+        outs = []
+        for t in range(row_blocks):
+            out = jnp.dot(lhs[t], f_hi[t], preferred_element_type=f32)
+            outs.append(out + jnp.dot(lhs[t], f_lo[t], preferred_element_type=f32))
+        for i in range(len(vectors)):
+            values = [out[2 * i : 2 * i + 1] + out[2 * i + 1 : 2 * i + 2] for out in outs]
+            for k in range(bands):
+                rows = []
+                for value in values:
                     for h in range(halves):
                         at = k * bs + h * LANES
-                        row = t * halves + h
-                        row_buf[phase, i * bands + k, my_row, row : row + 1, :] = value[
-                            :, at : at + LANES
-                        ]
-
-    def exchange_col(phase, rows):
+                        rows.append(value[:, at : at + LANES])
+                row_buf[phase, i * bands + k, my_row] = jnp.concatenate(rows, axis=0)
+
+    def start_col(phase, part, first, rows):
         copies = []
         for d in far_first(n_col):
-            mine = col_buf.at[phase, my_col, pl.ds(0, rows)]
+            mine = col_buf.at[phase, my_col, pl.ds(first, rows)]
             copies.append(
                 pltpu.make_async_remote_copy(
                     src_ref=mine,
                     dst_ref=mine,
-                    send_sem=col_send.at[phase, d],
-                    recv_sem=col_recv.at[phase, d],
+                    send_sem=col_send.at[phase, part, d],
+                    recv_sem=col_recv.at[phase, part, d],
                     device_id={"col": lax.rem(my_col + d, n_col)},
                 )
             )
             copies[-1].start()
         sends.extend(copies)
-        for copy in copies:
-            copy.wait_recv()
+        return copies
 
     def exchange_row(phase, first, last):
         copies = []
@@ -262,8 +270,7 @@
 
     col_phase = 0
     row_phase = 0
-    forward(x_ref, col_phase)
-    exchange_col(col_phase, 2 * tile)
+    forward(x_ref, col_phase, 0)
     total = col_sum(col_phase, 0, 2 * tile)
     g, a = total[0:tile], total[tile : 2 * tile]
     col_phase += 1
@@ -300,8 +307,7 @@
             col_buf[col_phase, my_col, at + 1 : at + 2, :] = lines(weighted * r)
             if inner > 0:
                 col_buf[col_phase, my_col, at + 2 : at + 3, :] = lines(weighted * p_ref[...])
-            forward(r_ref, col_phase)
-            exchange_col(col_phase, at + used)
+            forward(r_ref, col_phase, used)
             total = col_sum(col_phase, 0, at)
             sums = jnp.sum(col_sum(col_phase, at, at + used), axis=1, keepdims=True)
             col_phase += 1
@@ -355,7 +361,8 @@
         total = jnp.maximum(total, row_buf[row_phase, extra, i])
     for i, value in enumerate(dual):
         col_buf[col_phase, my_col, i : i + 1, :] = value
-    exchange_col(col_phase, ITERS)
+    for copy in start_col(col_phase, 0, 0, ITERS):
+        copy.wait_recv()
     found = col_buf[col_phase, 0, 0:ITERS]
     for i in range(1, n_col):
         found = jnp.maximum(found, col_buf[col_phase, i, 0:ITERS])
@@ -410,8 +417,8 @@
                 pltpu.VMEM((2 * bands, 2 * length, LANES), f32),
                 pltpu.VMEM((col_phases, n_col, 2 * tile + 8, LANES), f32),
                 pltpu.VMEM((row_phases, planes, n_row, tile, LANES), f32),
-                pltpu.SemaphoreType.DMA((col_phases, n_col)),
-                pltpu.SemaphoreType.DMA((col_phases, n_col)),
+                pltpu.SemaphoreType.DMA((col_phases, 2, n_col)),
+                pltpu.SemaphoreType.DMA((col_phases, 2, n_col)),
                 pltpu.SemaphoreType.DMA((row_phases, n_row)),
                 pltpu.SemaphoreType.DMA((row_phases, n_row)),
             ],

time: 66.5 us -> 66.5 us (level)
  no operation moved by 1% of the time
where the time goes in v4:
time: 66.5 us; the launch traced here: 66.4 us
  Pallas kernels  65.7 us (99%)
    pallas_call x1, Pallas kernels, local(): pl.pallas_call(functools.partial(kernel, n_row, n_col), name='osqp', out_...  64.2 us
    pallas_call x1, Pallas kernels, local(): pl.pallas_call(hand_over, name='hand_over', out_shape=tuple((jax.ShapeDty...  1.55 us

profile of v4, /device:TPU:0, one launch (start us, length us, event | category | flops | bytes accessed | tf_op | source)
XLA Modules:
  0.0 66.4 jit_solution(18200021948195758078)
XLA Ops:
  0.6 64.2 %osqp.1 = (f32[128,128]{1,0:T(8,128)}, f32[8,128]{1,0:T(8,128)}, f32[8,128]{1,0:T(8,128)}, f32[2,2]{1,0:T(2,128)}) custom-call(f32[4,2,256,256]{3,2,1,0:T(8,128)} %a_hbm.1, f32[4,2,256,256]{3,2,1,0:T(8,128)} %g_hbm.1, s32[1,2]{1,0:T(1,128)} %offsets_hbm.1, s32[2,4]{1,0:T(2,128)} %bitcast.18, f32[128,128]{1,0:T(8,128)} %bitcast.11, f32[128,128]{1,0:T(8,128)} %bitcast.12, ...), custom_call_target="tpu_custom_call" | custom-call | tf_op jit(solution)/shard_map/osqp/pallas_call | solution.py:390
  64.8 1.5 %hand_over.1 = (f32[128,128]{1,0:T(8,128)}, f32[8,128]{1,0:T(8,128)}, f32[8,128]{1,0:T(8,128)}, f32[2,2]{1,0:T(2,128)}) custom-call(f32[128,128]{1,0:T(8,128)} %get-tuple-element.12.refs_0_, f32[8,128]{1,0:T(8,128)} %get-tuple-element.13.refs_1_, f32[8,128]{1,0:T(8,128)} %get-tuple-element.14.refs_2_, f32[2,2]{1,0:T(2,128)} %get-tuple-element.15.refs_3_), custom_call_target="tpu_custom_call" | custom-call | tf_op jit(solution)/shard_map/hand_over/pallas_call | solution.py:429

commit v5 on v4

--- a/solution.py
+++ b/solution.py
@@ -164,7 +164,6 @@
                     pieces.append(ref[pl.ds(c * halves + h, 1), :])
             lhs.append(stacked([jnp.concatenate(pieces, axis=1)], line))
         dims = (((1,), (1,)), ((), ()))
-        copies = []
         for m in range(2):
             rows = []
             for t in range(row_blocks):
@@ -174,8 +173,7 @@
                 out = out[0:1] + out[1:2]
                 rows.extend(out[:, h * LANES : (h + 1) * LANES] for h in range(halves))
             col_buf[phase, my_col, m * tile : (m + 1) * tile, :] = jnp.concatenate(rows, axis=0)
-            copies.extend(start_col(phase, m, m * tile, tile + m * used))
-        for copy in copies:
+        for copy in start_col(phase, 0, 0, 2 * tile + used):
             copy.wait_recv()
 
     def backward(vectors, phase):
@@ -221,7 +219,7 @@
         sends.extend(copies)
         return copies
 
-    def exchange_row(phase, first, last):
+    def start_row(phase, first, last, part=0):
         copies = []
         for d in far_first(n_row):
             mine = row_buf.at[phase, pl.ds(first, last - first), my_row]
@@ -229,14 +227,17 @@
                 pltpu.make_async_remote_copy(
                     src_ref=mine,
                     dst_ref=mine,
-                    send_sem=row_send.at[phase, d],
-                    recv_sem=row_recv.at[phase, d],
+                    send_sem=row_send.at[phase, part, d],
+                    recv_sem=row_recv.at[phase, part, d],
                     device_id={"row": lax.rem(my_row + d, n_row)},
                 )
             )
             copies[-1].start()
         sends.extend(copies)
-        for copy in copies:
+        return copies
+
+    def exchange_row(phase, first, last):
+        for copy in start_row(phase, first, last):
             copy.wait_recv()
 
     def col_sum(phase, first, last):
@@ -287,11 +288,13 @@
         if outer > 0:
             vectors.append((g, y))
         backward(vectors, row_phase)
-        exchange_row(row_phase, 0, bands * len(vectors))
+        now = start_row(row_phase, 0, bands)
+        if outer > 0:
+            later = (start_row(row_phase, bands, 2 * bands, 1), row_phase)
+            primal.append(jnp.max(jnp.abs(a - z), axis=0, keepdims=True))
+        for copy in now:
+            copy.wait_recv()
         start_sum = expand(row_phase, 0)
-        if outer > 0:
-            primal.append(jnp.max(jnp.abs(a - z), axis=0, keepdims=True))
-            dual.append(dual_max(expand(row_phase, 1)))
         row_phase += 1
         x = x_ref[...]
         shifted = d_ref[...] + sigma_shift
@@ -328,7 +331,13 @@
                 backward([(g_d, rho_step * a_d)], row_phase)
                 exchange_row(row_phase, 0, extra + 1)
             else:
-                exchange_row(row_phase, extra, extra + 1)
+                now = start_row(row_phase, extra, extra + 1)
+                if outer > 0:
+                    for copy in later[0]:
+                        copy.wait_recv()
+                    dual.append(dual_max(expand(later[1], 1)))
+                for copy in now:
+                    copy.wait_recv()
             alpha = norm / (plane_sum(row_phase) + w_dir)
             p = p_ref[...]
             s_ref[...] = s_ref[...] + alpha * p
@@ -419,8 +428,8 @@
                 pltpu.VMEM((row_phases, planes, n_row, tile, LANES), f32),
                 pltpu.SemaphoreType.DMA((col_phases, 2, n_col)),
                 pltpu.SemaphoreType.DMA((col_phases, 2, n_col)),
-                pltpu.SemaphoreType.DMA((row_phases, n_row)),
-                pltpu.SemaphoreType.DMA((row_phases, n_row)),
+                pltpu.SemaphoreType.DMA((row_phases, 2, n_row)),
+                pltpu.SemaphoreType.DMA((row_phases, 2, n_row)),
             ],
             compiler_params=pltpu.CompilerParams(
                 collective_id=0, has_side_effects=True, vmem_limit_bytes=56 << 20

time: 66.5 us -> 67.8 us (1.020)
  Pallas kernels: 65.7 us -> 67 us
    pallas_call x1, Pallas kernels: 64.2 us -> 65.5 us  [local(): pl.pallas_call(functools.partial(kernel, n_row, n_col), name='osqp', out_...]
where the time goes in v5:
time: 67.8 us; the launch traced here: 67.6 us
  Pallas kernels  67 us (99%)
    pallas_call x1, Pallas kernels, local(): pl.pallas_call(functools.partial(kernel, n_row, n_col), name='osqp', out_...  65.5 us
    pallas_call x1, Pallas kernels, local(): pl.pallas_call(hand_over, name='hand_over', out_shape=tuple((jax.ShapeDty...  1.55 us

profile of v5, /device:TPU:0, one launch (start us, length us, event | category | flops | bytes accessed | tf_op | source)
XLA Modules:
  0.0 67.6 jit_solution(6241094387896537346)
XLA Ops:
  0.6 65.5 %osqp.1 = (f32[128,128]{1,0:T(8,128)}, f32[8,128]{1,0:T(8,128)}, f32[8,128]{1,0:T(8,128)}, f32[2,2]{1,0:T(2,128)}) custom-call(f32[4,2,256,256]{3,2,1,0:T(8,128)} %a_hbm.1, f32[4,2,256,256]{3,2,1,0:T(8,128)} %g_hbm.1, s32[1,2]{1,0:T(1,128)} %offsets_hbm.1, s32[2,4]{1,0:T(2,128)} %bitcast.18, f32[128,128]{1,0:T(8,128)} %bitcast.11, f32[128,128]{1,0:T(8,128)} %bitcast.12, ...), custom_call_target="tpu_custom_call" | custom-call | tf_op jit(solution)/shard_map/osqp/pallas_call | solution.py:399
  66.1 1.5 %hand_over.1 = (f32[128,128]{1,0:T(8,128)}, f32[8,128]{1,0:T(8,128)}, f32[8,128]{1,0:T(8,128)}, f32[2,2]{1,0:T(2,128)}) custom-call(f32[128,128]{1,0:T(8,128)} %get-tuple-element.12.refs_0_, f32[8,128]{1,0:T(8,128)} %get-tuple-element.13.refs_1_, f32[8,128]{1,0:T(8,128)} %get-tuple-element.14.refs_2_, f32[2,2]{1,0:T(2,128)} %get-tuple-element.15.refs_3_), custom_call_target="tpu_custom_call" | custom-call | tf_op jit(solution)/shard_map/hand_over/pallas_call | solution.py:438
